TPU v7x, 32 devices: a whole 2x2x4 slice. The times are simulated.
32 devices in a mesh: grp: 2 (over y), freq: 4 (over z), tm: 2 (over x), pol: 2 (over core).
Axes of the slice: x: 2, y: 2, z: 4, core: 2. Of those that a mesh axis runs over, the one named last changes fastest.
Arguments:
- voltages: bfloat16 [2, 8, 1024, 4, 2, 256], P('pol', ('grp', 'freq'), 'tm'), parts along dimension 1, may hold values from -6 to 6
- feed_gains: float32 [8, 2, 4, 2, 256], P(('grp', 'freq'), 'pol'), parts along dimension 0, may hold values from -5 to 5
- owner_table: int32 [64], replicated, may hold values from 0 to 3, as said below
- keep_flags: int32 [1024], replicated, may hold values 0 or 1
Outputs:
- owned: bfloat16 [128, 64, 2048], P(('grp', 'tm', 'pol'), None, 'freq'), parts along dimension 0
There are 2 independent parts, one for each index of `grp`. A program takes and returns all parts, laid end to end along the dimension named above; an argument that names none is the same for every part. Nothing has to cross between parts.
Inputs may be any that keep to these rules, and one draw needn't show every extreme that they name: `owner_table`: each index of freq owns from 0 to 32 beam sets; one owns exactly 32.
All inputs are finite; a program needn't handle non-finite values.
Results may differ from a plain program's by a relative error of at most 0.0058.
Values may be sent and summed in bfloat16 or wider, within the bound.
No kernel may reach another device: no remote copies, remote signals or barrier semaphores. Data moves between devices by JAX's collectives and lax.ppermute only.
A program may use at most 64 MiB of HBM per device.

v0:
```python
import jax
import jax.numpy as jnp
from jax import lax
from jax.sharding import PartitionSpec as P

NS = 256
CYL = 4
UPCH = 16
TAPS = 16
SET_BEAMS = 16


def shifted(block, axis, distance):
    devices = range(lax.axis_size(axis))
    route = [(i - distance, i) for i in devices if i - distance in devices]
    return lax.ppermute(block, axis, route)


def window_taps():
    span = TAPS * UPCH
    steps = jnp.arange(span, dtype=jnp.float32)
    weights = (
        jnp.sinc((steps - (span - 1) / 2.0) / UPCH) * jnp.sin(jnp.pi * (steps + 0.5) / span) ** 2
    )
    weights = weights / jnp.sqrt(jnp.sum(weights * weights))
    return weights.reshape(TAPS, UPCH)


def fine_tables():
    rows = jnp.arange(UPCH, dtype=jnp.int32)
    phase = rows[:, None] * rows[None, :] % UPCH
    angle = 2.0 * jnp.pi * phase.astype(jnp.float32) / UPCH
    return (jnp.cos(angle), jnp.sin(angle))


def beam_matrix():
    rows = jnp.arange(NS, dtype=jnp.int32)
    phase = rows[:, None] * rows[None, :] % NS
    angle = 2.0 * jnp.pi * phase.astype(jnp.float32) / NS
    scale = 1.0 / jnp.sqrt(jnp.float32(NS))
    cosine = jnp.cos(angle) * scale
    sine = jnp.sin(angle) * scale
    upper = jnp.concatenate([cosine, -sine], axis=1)
    lower = jnp.concatenate([sine, cosine], axis=1)
    return jnp.concatenate([upper, lower], axis=0).astype(jnp.bfloat16)


def cylinder_tables():
    rows = jnp.arange(CYL, dtype=jnp.int32)
    phase = rows[:, None] * rows[None, :] % CYL
    angle = 2.0 * jnp.pi * phase.astype(jnp.float32) / CYL
    return (0.5 * jnp.cos(angle), 0.5 * jnp.sin(angle))


def power_frames(frames, gain_pol, n_out):
    window = window_taps()
    fine_cos, fine_sin = fine_tables()
    beam_table = beam_matrix()
    cyl_cos, cyl_sin = cylinder_tables()
    highest = lax.Precision.HIGHEST
    chan_count = frames.shape[0]
    summed = jnp.zeros((chan_count, n_out) + frames.shape[2:], jnp.float32)
    for tap_index in range(TAPS):
        weights = window[tap_index].reshape(1, 1, UPCH, 1, 1, 1)
        summed = summed + weights * frames[:, tap_index : tap_index + n_out].astype(jnp.float32)
    real_part = summed[:, :, :, :, 0, :]
    imag_part = summed[:, :, :, :, 1, :]
    spec_real = jnp.einsum("qk,cmkxn->mcqxn", fine_cos, real_part, precision=highest) + jnp.einsum(
        "qk,cmkxn->mcqxn", fine_sin, imag_part, precision=highest
    )
    spec_imag = jnp.einsum("qk,cmkxn->mcqxn", fine_cos, imag_part, precision=highest) - jnp.einsum(
        "qk,cmkxn->mcqxn", fine_sin, real_part, precision=highest
    )
    gain_real = gain_pol[:, :, 0, :][None, :, None]
    gain_imag = gain_pol[:, :, 1, :][None, :, None]
    cal_real = spec_real * gain_real - spec_imag * gain_imag
    cal_imag = spec_real * gain_imag + spec_imag * gain_real
    calibrated = jnp.stack([cal_real, cal_imag], axis=4).astype(jnp.bfloat16)
    row_count = n_out * chan_count * UPCH
    flat = calibrated.reshape(row_count * CYL, 2 * NS)
    partial_value = jnp.dot(flat, beam_table, preferred_element_type=jnp.float32)
    partial_value = partial_value.reshape(row_count, CYL, 2, NS)
    beam_real = partial_value[:, :, 0, :]
    beam_imag = partial_value[:, :, 1, :]
    form_real = jnp.einsum("ec,rcn->ren", cyl_cos, beam_real, precision=highest) + jnp.einsum(
        "ec,rcn->ren", cyl_sin, beam_imag, precision=highest
    )
    form_imag = jnp.einsum("ec,rcn->ren", cyl_cos, beam_imag, precision=highest) - jnp.einsum(
        "ec,rcn->ren", cyl_sin, beam_real, precision=highest
    )
    powers = (form_real * form_real + form_imag * form_imag).astype(jnp.bfloat16)
    return powers.reshape(n_out, chan_count * UPCH, CYL * NS)


def slot_columns(owner_table, keep_flags, n_owner, most_sets):
    count = owner_table.shape[0]
    order = jnp.arange(count, dtype=jnp.int32)
    same_owner = owner_table[:, None] == owner_table[None, :]
    earlier = order[None, :] < order[:, None]
    set_rank = jnp.sum(jnp.logical_and(same_owner, earlier).astype(jnp.int32), axis=1)
    slot_index = owner_table * most_sets + set_rank
    places = jnp.arange(n_owner * most_sets, dtype=jnp.int32)
    matches = (slot_index[None, :] == places[:, None]).astype(jnp.int32)
    filled = jnp.sum(matches, axis=1)
    set_of = jnp.sum(matches * order[None, :], axis=1)
    within = jnp.arange(SET_BEAMS, dtype=jnp.int32)
    beam_index = (set_of[:, None] * SET_BEAMS + within[None, :]).reshape(-1)
    kept = jnp.take(keep_flags, beam_index).reshape(-1, SET_BEAMS)
    column_mask = (filled[:, None] * kept).reshape(-1)
    return (beam_index, column_mask)


def per_device(voltages, feed_gains, owner_table, keep_flags):
    samples = voltages[0]
    chan_count = samples.shape[0]
    frame_count = samples.shape[1] // UPCH
    frames = samples.reshape(chan_count, frame_count, UPCH, CYL, 2, NS)
    gain_pol = feed_gains[:, 0]
    history = TAPS - 1
    tail_frames = frames[:, frame_count - history :]
    before = shifted(tail_frames, "tm", 1)
    joined = jnp.concatenate([before, frames], axis=1)
    powers = power_frames(joined, gain_pol, frame_count)
    n_owner = lax.axis_size("freq")
    most_sets = 2 * owner_table.shape[0] // n_owner
    beam_index, column_mask = slot_columns(owner_table, keep_flags, n_owner, most_sets)
    mask_values = column_mask.astype(jnp.bfloat16)[None, None, :]
    summed = (
        lax.psum_scatter(powers, "pol", scatter_dimension=0, tiled=True)
        .astype(jnp.float32)
        .astype(jnp.bfloat16)
    )
    outgoing = jnp.take(summed, beam_index, axis=2) * mask_values
    return lax.all_to_all(outgoing, "freq", split_axis=2, concat_axis=1, tiled=True)


def solution(mesh):
    return jax.shard_map(
        per_device,
        mesh=mesh,
        in_specs=(
            P("pol", ("grp", "freq"), "tm", None, None, None),
            P(("grp", "freq"), "pol", None, None, None),
            P(),
            P(),
        ),
        out_specs=P(("grp", "tm", "pol"), None, "freq"),
        check_vma=False,
    )
```

profile of v0, /device:TPU:0, one launch (start us, length us, event | category | flops | bytes accessed | tf_op | source)
XLA Modules:
  0.0 210.3 jit_solution(8894756028634160894)
XLA Ops:
  6.5 2.0 copy.21
  9.7 5.8 %collective-permute-start = (bf16[1,15,16,4,2,256]{5,2,3,1,4,0:T(8,128)(2,1)}, bf16[1,15,16,4,2,256]{5,2,3,1,4,0:T(8,128)(2,1)}, u32[]{:S(2)}, u32[]{:S(2)}) collective-permute-start(bf16[1,15,16,4,2,256]{5,2,3,1,4,0:T(8,128)(2,1)} %copy.53), channel_id=1, source_target_pairs={{0,2},{1,3},{4,6},{5,7},{8,10},{9,11},{12,14},{13,15},{16,18},{17,... | collective-permute-start | bytes 2949128 | tf_op jit(solution)/shard_map/ppermute | solution.py:16
  19.1 16.8 %collective-permute-done = bf16[1,15,16,4,2,256]{5,2,3,1,4,0:T(8,128)(2,1)} collective-permute-done((bf16[1,15,16,4,2,256]{5,2,3,1,4,0:T(8,128)(2,1)}, bf16[1,15,16,4,2,256]{5,2,3,1,4,0:T(8,128)(2,1)}, u32[]{:S(2)}, u32[]{:S(2)}) %collective-permute-start) | collective-permute-done | bytes 983072 | tf_op jit(solution)/shard_map/ppermute | solution.py:16
  35.9 1.3 constant_dynamic-update-slice_fusion.1
  37.5 8.6 %multiply_add_fusion = f32[1,32,16,4,2,256]{5,2,3,1,4,0:T(8,128)S(1)} fusion(bf16[1,47,16,4,2,256]{5,2,3,1,4,0:T(8,128)(2,1)S(1)} %constant_dynamic-update-slice_fusion, f32[16]{0:T(128)S(1)} %get-tuple-element.16, f32[16]{0:T(128)S(1)} %get-tuple-element.17, f32[16]{0:T(128)S(1)} %get-tuple-element.18, f32[16]{0:T(128)S(1)} %get-tuple-element.19, ...), kind=kLoop, calls=%fused_computation.3 | loop fusion | flops 49283072 | bytes 37749760 | tf_op jit(solution)/shard_map/add | solution.py:65
  46.1 2.0 fusion.6
  48.1 1.9 fusion.9
  50.0 2.0 fusion.21
  52.0 2.6 %fusion.26 = (bf16[32,1,16,4,1,256]{5,2,3,0,4,1:T(8,128)(2,1)S(1)}, bf16[32,1,16,4,1,256]{5,2,3,0,4,1:T(8,128)(2,1)S(1)}) fusion(f32[32,4,256,16]{2,3,1,0:T(8,128)S(1)} %fusion.21, f32[4,256]{1,0:T(4,128)S(1)} %get-tuple-element.33, f32[4,256]{1,0:T(4,128)S(1)} %get-tuple-element.34, f32[32,4,256,16]{2,3,1,0:T(8,128)S(1)} %fusion.6, ...), kind=kOutput, calls=%fused_computation.36 | convolution fusion | flops 105385472 | bytes 8396800 | tf_op jit(solution)/shard_map/qk,cmkxn->mcqxn/dot_general | solution.py:71
  54.9 4.8 %copy.25 = bf16[32,1,16,4,2,256]{5,4,2,0,3,1:T(2,128)(2,1)} copy(bf16[32,1,16,4,2,256]{5,2,3,0,4,1:T(8,128)(2,1)S(1)} %pad_maximum_fusion) | data formatting | bytes 4194304 | tf_op jit(solution)/shard_map/stack | solution.py:78
  59.7 3.2 %reshape.273 = bf16[512,4,512,1]{2,0,1,3:T(8,128)(2,1)S(1)} reshape(bf16[32,1,16,4,2,256]{5,4,2,0,3,1:T(2,128)(2,1)} %copy.25) | data formatting | bytes 4194304 | tf_op jit(solution)/shard_map/convert_element_type | solution.py:78
  64.4 4.4 %fusion.10 = f32[512,256,4]{1,2,0:T(4,128)S(1)} fusion(f32[512,4,256]{2,0,1:T(8,128)S(1)} %get-tuple-element.12), kind=kOutput, calls=%fused_computation.24 | convolution fusion | flops 25166064 | bytes 4194304 | tf_op jit(solution)/shard_map/ec,rcn->ren/dot_general | solution.py:88
  68.8 4.4 %fusion.12 = f32[512,256,4]{1,2,0:T(4,128)S(1)} fusion(f32[512,4,256]{2,0,1:T(8,128)S(1)} %get-tuple-element.12), kind=kOutput, calls=%fused_computation.26 | convolution fusion | flops 25166064 | bytes 4194304 | tf_op jit(solution)/shard_map/ec,rcn->ren/dot_general | solution.py:85
  73.2 4.4 %fusion.14 = f32[512,256,4]{1,2,0:T(4,128)S(1)} fusion(f32[512,4,256]{2,0,1:T(8,128)S(1)} %get-tuple-element.11), kind=kOutput, calls=%fused_computation.28 | convolution fusion | flops 25166064 | bytes 4194304 | tf_op jit(solution)/shard_map/ec,rcn->ren/dot_general | solution.py:88
  77.6 5.5 %fusion.22 = bf16[512,4,256]{2,1,0:T(4,128)(2,1)S(1)} fusion(f32[512,256,4]{1,2,0:T(4,128)S(1)} %fusion.10, f32[512,256,4]{1,2,0:T(4,128)S(1)} %fusion.14, f32[512,256,4]{1,2,0:T(4,128)S(1)} %fusion.12, f32[512,4,256]{2,0,1:T(8,128)S(1)} %get-tuple-element.11), kind=kOutput, calls=%fused_computation.34 | convolution fusion | flops 28311792 | bytes 9437184 | tf_op jit(solution)/shard_map/ec,rcn->ren/dot_general | solution.py:85
  83.9 12.3 %copy.30 = bf16[32,16,1024]{1,0,2:T(8,128)(2,1)} copy(bf16[32,16,1024]{2,1,0:T(8,128)(2,1)S(1)} %reshape.254) | data formatting | bytes 2097152 | tf_op jit(solution)/shard_map/reshape | solution.py:92
  97.6 8.6 %gather_fusion.1 = s32[2048]{0:T(1024)S(1)} fusion(s32[1024]{0:T(1024)S(1)} %copy-done, s32[2048]{0:T(1024)S(1)} %broadcast_clamp_fusion), kind=kCustom, calls=%fused_computation.1 | custom fusion | bytes 24576 | tf_op jit(solution)/shard_map/jit(_take)/gather | solution.py:108
  106.2 8.6 %reduce-scatter.2.cloned.1.call-done = bf16[16,16,1024]{1,0,2:T(8,128)(2,1)} async-done(((bf16[32,16,1024]{1,0,2:T(8,128)(2,1)}), bf16[16,16,1024]{1,0,2:T(8,128)(2,1)}) %reduce-scatter.2.cloned.1.call-update) | async-done | bytes 524304 | tf_op jit(solution)/shard_map/reduce_scatter | solution.py:129
  114.8 18.4 %gather_fusion = bf16[2048,16,16]{2,1,0:T(8,128)(2,1)} fusion(bf16[16,16,1024]{1,0,2:T(8,128)(2,1)} %reduce-scatter.2.cloned.1.call-done, s32[2048]{0:T(1024)S(1)} %broadcast_clamp_fusion), kind=kCustom, calls=%fused_computation | custom fusion | bytes 2105344 | tf_op jit(solution)/shard_map/jit(_take)/gather | solution.py:133
  133.2 13.1 %fusion.117 = bf16[2048,16,16]{2,1,0:T(8,128)(2,1)} fusion(bf16[2048]{0:T(1024)(128)(2,1)S(1)} %get-tuple-element.7, bf16[2048,16,16]{2,1,0:T(8,128)(2,1)} %gather_fusion, pred[2048]{0:T(1024)(128)(4,1)S(1)} %get-tuple-element.8), kind=kLoop, calls=%fused_computation.161 | loop fusion | flops 1048576 | bytes 2103296
  146.3 10.2 %reshape.278 = bf16[4,2,65536]{2,1,0:T(2,128)(2,1)S(1)} reshape(bf16[2048,16,16]{2,1,0:T(8,128)(2,1)} %fusion.117) | data formatting | bytes 2097152
  156.6 30.8 %all_to_all.18 = bf16[4,2,65536]{2,1,0:T(2,128)(2,1)S(1)} all-to-all(bf16[4,2,65536]{2,1,0:T(2,128)(2,1)S(1)} %reshape.278), channel_id=1, replica_groups=mesh['grp'=2,'freq'=4,'tm'=2,'pol'=2] {'freq'}, dimensions={0} | all-to-all | bytes 2097152 | tf_op jit(solution)/shard_map/all_to_all | solution.py:134
  187.4 6.9 %reshape.279 = bf16[2048,16,16]{2,1,0:T(8,128)(2,1)} reshape(bf16[4,2,65536]{2,1,0:T(2,128)(2,1)S(1)} %all_to_all.18) | data formatting | bytes 2097152
  194.3 9.1 %copy.31 = bf16[16,4,16,512]{3,2,1,0:T(8,128)(2,1)} copy(bf16[16,4,16,512]{2,0,3,1:T(8,128)(2,1)} %bitcast.109) | data formatting | bytes 2097152 | tf_op jit(solution)/shard_map/all_to_all | solution.py:134
  (35 shorter events, 8.3 us)
Async XLA Ops:
  6.5 91.0 %copy-start = (s32[1024]{0:T(1024)S(1)}, s32[1024]{0:T(1024)}, u32[]{:S(2)}) copy-start(s32[1024]{0:T(1024)} %param.7) | copy-start | bytes 12292
  6.5 108.3 %reduce-scatter.2.cloned.1.call-start = ((), (), s32[]{:S(2)}) async-start(), calls=%async_computation.2 | async-start | bytes 12582912 | tf_op jit(solution)/shard_map/reduce_scatter | solution.py:129
  8.6 10.5 %copy-start.1 = (f32[1,1,4,2,256]{4,3,2,1,0:T(2,128)S(1)}, f32[1,1,4,2,256]{4,3,2,1,0:T(2,128)}, u32[]{:S(2)}) copy-start(f32[1,1,4,2,256]{4,3,2,1,0:T(2,128)} %param.5) | copy-start | bytes 24580
  9.7 26.2 %collective-permute-start = (bf16[1,15,16,4,2,256]{5,2,3,1,4,0:T(8,128)(2,1)}, bf16[1,15,16,4,2,256]{5,2,3,1,4,0:T(8,128)(2,1)}, u32[]{:S(2)}, u32[]{:S(2)}) collective-permute-start(bf16[1,15,16,4,2,256]{5,2,3,1,4,0:T(8,128)(2,1)} %copy.53), channel_id=1, source_target_pairs={{0,2},{1,3},{4,6},{5,7},{8,10},{9,11},{12,14},{13,15},{16,18},{17,... | collective-permute-start | bytes 2949128 | tf_op jit(solution)/shard_map/ppermute | solution.py:16
  96.2 0.7 copy-start.2
Sparse Core Ops, SparseCore 0:
  96.3 18.4 reduce-scatter.1
where the time goes:
time: 211 us; the launch traced here: 210 us
  local copies, waits for them, and re-layouts  80.3 us (38%)
  blocking collectives  30.8 us (15%)
  matrix products  28.5 us (14%)
  waiting for transfers between devices  25.5 us (12%)
  other arithmetic  25.1 us (12%)
  between operations  14.3 us (7%)
  starting transfers between devices  5.82 us (3%)
    all_to_all x1, blocking collectives, per_device(): lax.all_to_all(outgoing, 'freq', split_axis=2, concat_axis=1, tiled=True)  30.8 us
    unnamed x12, local copies, waits for them, and re-layouts  22.2 us
    gather x1, local copies, waits for them, and re-layouts, per_device(): outgoing = jnp.take(summed, beam_index, axis=2) * mask_values  18.4 us
    ppermute x1, waiting for transfers between devices, shifted(): return lax.ppermute(block, axis, route)  16.8 us
    unnamed x1, other arithmetic  13.1 us
    reshape x2, local copies, waits for them, and re-layouts, power_frames(): return powers.reshape(n_out, chan_count * UPCH, CYL * NS)  13 us
    all_to_all x1, local copies, waits for them, and re-layouts, per_device(): lax.all_to_all(outgoing, 'freq', split_axis=2, concat_axis=1, tiled=True)  9.1 us
    reduce_scatter x1, waiting for transfers between devices, per_device(): lax.psum_scatter(powers, 'pol', scatter_dimension=0, tiled=True)  8.64 us
  transfers between devices with their start and end apart: 2, of which 2 were waited for; matrix products, arithmetic and copies ran while one was open for 6% of the time, Pallas kernels for 0%

commit v1 on v0

--- a/solution.py
+++ b/solution.py
@@ -8,6 +8,13 @@
 UPCH = 16
 TAPS = 16
 SET_BEAMS = 16
+
+
+def swap_blocks(value, mesh_axis, split, join):
+    size = lax.axis_size(mesh_axis)
+    blocks = jnp.stack(jnp.split(value, size, axis=split), axis=0)
+    blocks = lax.all_to_all(blocks, mesh_axis, split_axis=0, concat_axis=0)
+    return jnp.concatenate(blocks, axis=join)
 
 
 def shifted(block, axis, distance):
@@ -131,7 +138,7 @@
         .astype(jnp.bfloat16)
     )
     outgoing = jnp.take(summed, beam_index, axis=2) * mask_values
-    return lax.all_to_all(outgoing, "freq", split_axis=2, concat_axis=1, tiled=True)
+    return swap_blocks(outgoing, "freq", 2, 1)
 
 
 def solution(mesh):

time: 211 us -> 197 us (0.934)
  local copies, waits for them, and re-layouts: 80.3 us -> 67.1 us
    unnamed x12 -> x10, local copies, waits for them, and re-layouts: 22.2 us -> 5.02 us
    unnamed x1 -> x0, other arithmetic: 13.1 us -> none
    mul x0 -> x1, other arithmetic: none -> 12.3 us  [per_device(): outgoing = jnp.take(summed, beam_index, axis=2) * mask_values]
    another operation x0 -> x5, local copies, waits for them, and re-layouts: none -> 12 us  [swap_blocks(): blocks = jnp.stack(jnp.split(value, size, axis=split), axis=0)]
    all_to_all x1, local copies, waits for them, and re-layouts: 9.1 us -> 1.06 us  [swap_blocks(): blocks = lax.all_to_all(blocks, mesh_axis, split_axis=0, concat_axis=0)]
where the time goes in v1:
time: 197 us; the launch traced here: 196 us
  local copies, waits for them, and re-layouts  67.1 us (34%)
  blocking collectives  30.8 us (16%)
  matrix products  28.5 us (14%)
  waiting for transfers between devices  25.4 us (13%)
  other arithmetic  24.5 us (12%)
  between operations  14.3 us (7%)
  starting transfers between devices  5.83 us (3%)
    all_to_all x1, blocking collectives, swap_blocks(): blocks = lax.all_to_all(blocks, mesh_axis, split_axis=0, concat_axis=0)  30.8 us
    gather x1, local copies, waits for them, and re-layouts, per_device(): outgoing = jnp.take(summed, beam_index, axis=2) * mask_values  18.3 us
    ppermute x1, waiting for transfers between devices, shifted(): return lax.ppermute(block, axis, route)  16.8 us
    reshape x2, local copies, waits for them, and re-layouts, power_frames(): return powers.reshape(n_out, chan_count * UPCH, CYL * NS)  13 us
    mul x1, other arithmetic, per_device(): outgoing = jnp.take(summed, beam_index, axis=2) * mask_values  12.3 us
    another operation x5, local copies, waits for them, and re-layouts, swap_blocks(): blocks = jnp.stack(jnp.split(value, size, axis=split), axis=0)  12 us
    reduce_scatter x1, waiting for transfers between devices, per_device(): lax.psum_scatter(powers, 'pol', scatter_dimension=0, tiled=True)  8.64 us
    add x1, other arithmetic, power_frames(): summed + weights * frames[:, tap_index:tap_index + n_out].astype(jnp.floa...  8.6 us
  transfers between devices with their start and end apart: 2, of which 2 were waited for; matrix products, arithmetic and copies ran while one was open for 6% of the time, Pallas kernels for 0%

profile of v1, /device:TPU:0, one launch (start us, length us, event | category | flops | bytes accessed | tf_op | source)
XLA Modules:
  0.0 196.3 jit_solution(11209824515324255149)
XLA Ops:
  6.5 2.0 %copy.46 = bf16[1,1,512,4,2,256]{5,2,4,3,1,0:T(8,128)(2,1)S(1)} copy(bf16[1,1,512,4,2,256]{5,4,3,2,1,0:T(2,128)(2,1)} %param.4) | data formatting | bytes 4194304 | tf_op args[0]
  9.7 5.8 %collective-permute-start = (bf16[1,15,16,4,2,256]{5,2,3,1,4,0:T(8,128)(2,1)}, bf16[1,15,16,4,2,256]{5,2,3,1,4,0:T(8,128)(2,1)}, u32[]{:S(2)}, u32[]{:S(2)}) collective-permute-start(bf16[1,15,16,4,2,256]{5,2,3,1,4,0:T(8,128)(2,1)} %copy.82), channel_id=1, source_target_pairs={{0,2},{1,3},{4,6},{5,7},{8,10},{9,11},{12,14},{13,15},{16,18},{17,... | collective-permute-start | bytes 2949128 | tf_op jit(solution)/shard_map/ppermute | solution.py:23
  19.2 16.8 %collective-permute-done = bf16[1,15,16,4,2,256]{5,2,3,1,4,0:T(8,128)(2,1)} collective-permute-done((bf16[1,15,16,4,2,256]{5,2,3,1,4,0:T(8,128)(2,1)}, bf16[1,15,16,4,2,256]{5,2,3,1,4,0:T(8,128)(2,1)}, u32[]{:S(2)}, u32[]{:S(2)}) %collective-permute-start) | collective-permute-done | bytes 983072 | tf_op jit(solution)/shard_map/ppermute | solution.py:23
  37.5 8.6 %multiply_add_fusion = f32[1,32,16,4,2,256]{5,2,3,1,4,0:T(8,128)S(1)} fusion(bf16[1,47,16,4,2,256]{5,2,3,1,4,0:T(8,128)(2,1)S(1)} %constant_dynamic-update-slice_fusion, f32[16]{0:T(128)S(1)} %get-tuple-element.20, f32[16]{0:T(128)S(1)} %get-tuple-element.21, f32[16]{0:T(128)S(1)} %get-tuple-element.22, f32[16]{0:T(128)S(1)} %get-tuple-element.23, ...), kind=kLoop, calls=%fused_computation.3 | loop fusion | flops 49283072 | bytes 37749760 | tf_op jit(solution)/shard_map/add | solution.py:72
  46.1 2.0 %fusion.6 = f32[32,4,256,16]{2,3,1,0:T(8,128)S(1)} fusion(f32[1,32,16,4,2,256]{5,2,3,1,4,0:T(8,128)S(1)} %multiply_add_fusion), kind=kOutput, calls=%fused_computation.24 | convolution fusion | flops 100666880 | bytes 4194304 | tf_op jit(solution)/shard_map/qk,cmkxn->mcqxn/dot_general | solution.py:78
  48.1 1.9 fusion.9
  50.0 2.0 %fusion.21 = f32[32,4,256,16]{2,3,1,0:T(8,128)S(1)} fusion(f32[32,4,256,16]{2,3,1,0:T(8,128)S(1)} %fusion.9, f32[1,32,16,4,2,256]{5,2,3,1,4,0:T(8,128)S(1)} %multiply_add_fusion), kind=kOutput, calls=%fused_computation.37 | convolution fusion | flops 101191168 | bytes 6291456 | tf_op jit(solution)/shard_map/qk,cmkxn->mcqxn/dot_general | solution.py:75
  52.0 2.6 %fusion.26 = (bf16[32,1,16,4,1,256]{5,2,3,0,4,1:T(8,128)(2,1)S(1)}, bf16[32,1,16,4,1,256]{5,2,3,0,4,1:T(8,128)(2,1)S(1)}) fusion(f32[32,4,256,16]{2,3,1,0:T(8,128)S(1)} %fusion.21, f32[4,256]{1,0:T(4,128)S(1)} %get-tuple-element.37, f32[4,256]{1,0:T(4,128)S(1)} %get-tuple-element.38, f32[32,4,256,16]{2,3,1,0:T(8,128)S(1)} %fusion.6, ...), kind=kOutput, calls=%fused_computation.40 | convolution fusion | flops 105385472 | bytes 8396800 | tf_op jit(solution)/shard_map/qk,cmkxn->mcqxn/dot_general | solution.py:78
  54.9 4.8 %copy.50 = bf16[32,1,16,4,2,256]{5,4,2,0,3,1:T(2,128)(2,1)} copy(bf16[32,1,16,4,2,256]{5,2,3,0,4,1:T(8,128)(2,1)S(1)} %pad_maximum_fusion) | data formatting | bytes 4194304 | tf_op jit(solution)/shard_map/stack | solution.py:85
  59.7 3.2 %reshape.281 = bf16[512,4,512,1]{2,0,1,3:T(8,128)(2,1)S(1)} reshape(bf16[32,1,16,4,2,256]{5,4,2,0,3,1:T(2,128)(2,1)} %copy.50) | data formatting | bytes 4194304 | tf_op jit(solution)/shard_map/convert_element_type | solution.py:85
  64.4 4.4 %fusion.10 = f32[512,256,4]{1,2,0:T(4,128)S(1)} fusion(f32[512,4,256]{2,0,1:T(8,128)S(1)} %get-tuple-element.16), kind=kOutput, calls=%fused_computation.28 | convolution fusion | flops 25166064 | bytes 4194304 | tf_op jit(solution)/shard_map/ec,rcn->ren/dot_general | solution.py:95
  68.8 4.4 %fusion.12 = f32[512,256,4]{1,2,0:T(4,128)S(1)} fusion(f32[512,4,256]{2,0,1:T(8,128)S(1)} %get-tuple-element.16), kind=kOutput, calls=%fused_computation.30 | convolution fusion | flops 25166064 | bytes 4194304 | tf_op jit(solution)/shard_map/ec,rcn->ren/dot_general | solution.py:92
  73.2 4.4 %fusion.14 = f32[512,256,4]{1,2,0:T(4,128)S(1)} fusion(f32[512,4,256]{2,0,1:T(8,128)S(1)} %get-tuple-element.15), kind=kOutput, calls=%fused_computation.32 | convolution fusion | flops 25166064 | bytes 4194304 | tf_op jit(solution)/shard_map/ec,rcn->ren/dot_general | solution.py:95
  77.6 5.5 %fusion.22 = bf16[512,4,256]{2,1,0:T(4,128)(2,1)S(1)} fusion(f32[512,256,4]{1,2,0:T(4,128)S(1)} %fusion.10, f32[512,256,4]{1,2,0:T(4,128)S(1)} %fusion.14, f32[512,256,4]{1,2,0:T(4,128)S(1)} %fusion.12, f32[512,4,256]{2,0,1:T(8,128)S(1)} %get-tuple-element.15), kind=kOutput, calls=%fused_computation.38 | convolution fusion | flops 28311792 | bytes 9437184 | tf_op jit(solution)/shard_map/ec,rcn->ren/dot_general | solution.py:92
  83.9 12.2 %copy.55 = bf16[32,16,1024]{1,0,2:T(8,128)(2,1)} copy(bf16[32,16,1024]{2,1,0:T(8,128)(2,1)S(1)} %reshape.260) | data formatting | bytes 2097152 | tf_op jit(solution)/shard_map/reshape | solution.py:99
  97.6 8.6 %gather_fusion.1 = s32[2048]{0:T(1024)S(1)} fusion(s32[1024]{0:T(1024)S(1)} %copy-done, s32[2048]{0:T(1024)S(1)} %broadcast_clamp_fusion), kind=kCustom, calls=%fused_computation.1 | custom fusion | bytes 24576 | tf_op jit(solution)/shard_map/jit(_take)/gather | solution.py:115
  106.2 8.6 %reduce-scatter.2.cloned.1.call-done = bf16[16,16,1024]{1,0,2:T(8,128)(2,1)} async-done(((bf16[32,16,1024]{1,0,2:T(8,128)(2,1)}), bf16[16,16,1024]{1,0,2:T(8,128)(2,1)}) %reduce-scatter.2.cloned.1.call-update) | async-done | bytes 524304 | tf_op jit(solution)/shard_map/reduce_scatter | solution.py:136
  114.8 18.3 %gather_fusion = bf16[2048,16,16]{2,1,0:T(8,128)(2,1)} fusion(bf16[16,16,1024]{1,0,2:T(8,128)(2,1)} %reduce-scatter.2.cloned.1.call-done, s32[2048]{0:T(1024)S(1)} %broadcast_clamp_fusion), kind=kCustom, calls=%fused_computation | custom fusion | bytes 2105344 | tf_op jit(solution)/shard_map/jit(_take)/gather | solution.py:140
  133.1 12.3 %multiply_bitcast_fusion = bf16[16,16,2048]{1,0,2:T(8,128)(2,1)S(1)} fusion(bf16[2048,16,16]{2,1,0:T(8,128)(2,1)} %gather_fusion, pred[2048]{0:T(1024)(128)(4,1)S(1)} %get-tuple-element.8, bf16[2048]{0:T(1024)(128)(2,1)S(1)} %get-tuple-element.7), kind=kLoop, calls=%fused_computation.2 | loop fusion | flops 1048576 | bytes 2103296 | tf_op jit(solution)/shard_map/mul | solution.py:140
  145.4 3.0 %slice_bitcast_fusion.3 = (bf16[1,16,16,512]{2,1,3,0:T(8,128)(2,1)}, bf16[1,16,16,512]{2,1,3,0:T(8,128)(2,1)}, bf16[1,16,16,512]{2,1,3,0:T(8,128)(2,1)}, bf16[1,16,16,512]{2,1,3,0:T(8,128)(2,1)S(1)}) fusion(bf16[16,16,2048]{1,0,2:T(8,128)(2,1)S(1)} %multiply_bitcast_fusion), kind=kLoop, calls=%fused_computation.7 | loop fusion | bytes 2097152 | tf_op jit(solution)/shard_map/stack | solution.py:15
  148.4 2.5 %copy.56 = bf16[1,16,16,512]{3,2,1,0:T(8,128)(2,1)S(1)} copy(bf16[1,16,16,512]{2,1,3,0:T(8,128)(2,1)} %get-tuple-element.9) | data formatting | bytes 524288 | tf_op jit(solution)/shard_map/stack | solution.py:15
  150.9 2.5 %copy.59 = bf16[1,16,16,512]{3,2,1,0:T(8,128)(2,1)S(1)} copy(bf16[1,16,16,512]{2,1,3,0:T(8,128)(2,1)} %get-tuple-element.10) | data formatting | bytes 524288 | tf_op jit(solution)/shard_map/stack | solution.py:15
  153.4 2.5 %copy.58 = bf16[1,16,16,512]{3,2,1,0:T(8,128)(2,1)S(1)} copy(bf16[1,16,16,512]{2,1,3,0:T(8,128)(2,1)} %get-tuple-element.11) | data formatting | bytes 524288 | tf_op jit(solution)/shard_map/stack | solution.py:15
  157.6 30.8 %all_to_all.5 = bf16[4,16,16,512]{3,2,1,0:T(8,128)(2,1)S(1)} all-to-all(bf16[4,16,16,512]{3,2,1,0:T(8,128)(2,1)S(1)} %pad_maximum_fusion.1), channel_id=1, replica_groups=mesh['grp'=2,'freq'=4,'tm'=2,'pol'=2] {'freq'}, dimensions={0} | all-to-all | bytes 2097152 | tf_op jit(solution)/shard_map/all_to_all | solution.py:16
  (39 shorter events, 12.4 us)
Async XLA Ops:
  6.5 91.0 %copy-start = (s32[1024]{0:T(1024)S(1)}, s32[1024]{0:T(1024)}, u32[]{:S(2)}) copy-start(s32[1024]{0:T(1024)} %param.7) | copy-start | bytes 12292
  6.5 108.3 %reduce-scatter.2.cloned.1.call-start = ((), (), s32[]{:S(2)}) async-start(), calls=%async_computation.2 | async-start | bytes 12582912 | tf_op jit(solution)/shard_map/reduce_scatter | solution.py:136
  8.7 10.5 %copy-start.1 = (f32[1,1,4,2,256]{4,3,2,1,0:T(2,128)S(1)}, f32[1,1,4,2,256]{4,3,2,1,0:T(2,128)}, u32[]{:S(2)}) copy-start(f32[1,1,4,2,256]{4,3,2,1,0:T(2,128)} %param.5) | copy-start | bytes 24580
  9.7 26.2 %collective-permute-start = (bf16[1,15,16,4,2,256]{5,2,3,1,4,0:T(8,128)(2,1)}, bf16[1,15,16,4,2,256]{5,2,3,1,4,0:T(8,128)(2,1)}, u32[]{:S(2)}, u32[]{:S(2)}) collective-permute-start(bf16[1,15,16,4,2,256]{5,2,3,1,4,0:T(8,128)(2,1)} %copy.82), channel_id=1, source_target_pairs={{0,2},{1,3},{4,6},{5,7},{8,10},{9,11},{12,14},{13,15},{16,18},{17,... | collective-permute-start | bytes 2949128 | tf_op jit(solution)/shard_map/ppermute | solution.py:23
  96.1 0.7 copy-start.2
Sparse Core Ops, SparseCore 0:
  96.3 18.4 reduce-scatter.1
